TPU v7x, 32 devices: a whole 2x2x4 slice. The times are simulated.
32 devices in a mesh: dp: 16 (over z, y, x), mp: 2 (over core).
Axes of the slice: x: 2, y: 2, z: 4, core: 2. Of those that a mesh axis runs over, the one named last changes fastest.
Arguments:
- inputs: bfloat16 [32768, 4096], P('dp', 'mp'), may hold values from -6 to 6
- cotangents: bfloat16 [32768, 4096], P('dp', 'mp'), may hold values from -6 to 6
- loss_token_mask: int32 [32768], P('dp'), may hold values 0 or 1
- adapter_down_weight: bfloat16 [128, 4096], P(None, 'mp'), may hold values from -0.09375 to 0.09375
- adapter_up_weight: bfloat16 [4096, 128], P('mp'), may hold values from -0.5 to 0.5
- width_projection: bfloat16 [2, 4096, 256], P(None, 'mp'), may hold values from -0.09375 to 0.09375
- rank_projection: bfloat16 [2, 128, 16], replicated, may hold values from -0.5 to 0.5
- targets: float32 [64, 8192], P(None, ('dp', 'mp')), may hold values from -500 to 500
Outputs:
- scores: float32 [128, 64], P('dp')
All inputs are finite; a program needn't handle non-finite values. No bound on the sum of `loss_token_mask` on one device may be relied on, other than what follows from the above.
Results may differ from a plain program's by a relative error of at most 0.0003.
Values sent between devices are 32-bit elements; how exact they have to be, the bound alone decides.
A program may use at most 64 MiB of HBM per device.

v0:
```python
import math

import jax
import jax.numpy as jnp
from jax import lax
from jax.sharding import PartitionSpec as P

SEQ = 256
KP = 256
KQ = 16
FEAT = 8192


adapter_scale = 4.0
epsilon = 1e-06


def on_device(
    inputs,
    cotangents,
    loss_token_mask,
    adapter_down_weight,
    adapter_up_weight,
    width_projection,
    rank_projection,
    targets,
):
    samples = inputs.shape[0] // SEQ
    masked_gradient = cotangents * loss_token_mask.astype(jnp.bfloat16)[:, None]
    cols_first = rank_projection[0].astype(jnp.float32)
    cols_second = rank_projection[1].astype(jnp.float32)
    down_partial_gradient = jnp.dot(
        inputs, adapter_down_weight.T, preferred_element_type=jnp.float32
    )
    up_partial_gradient = jnp.dot(
        masked_gradient, adapter_up_weight, preferred_element_type=jnp.float32
    )
    down_rank_product, up_rank_product = lax.psum(
        (down_partial_gradient, up_partial_gradient), "mp"
    )
    compact_up_gradient = jnp.dot(up_rank_product, cols_first, precision=lax.Precision.HIGHEST)
    compact_down_gradient = jnp.dot(down_rank_product, cols_second, precision=lax.Precision.HIGHEST)
    projected_activations = jnp.dot(
        inputs, width_projection[0], preferred_element_type=jnp.float32
    ).reshape(samples, SEQ, KP)
    projected_masked_gradient = jnp.dot(
        masked_gradient, width_projection[1], preferred_element_type=jnp.float32
    ).reshape(samples, SEQ, KP)
    first_matrix = adapter_scale * jnp.einsum(
        "stk,stq->skq",
        projected_activations,
        compact_up_gradient.reshape(samples, SEQ, KQ),
        precision=lax.Precision.HIGHEST,
    )
    second_matrix = adapter_scale * jnp.einsum(
        "stk,stq->skq",
        projected_masked_gradient,
        compact_down_gradient.reshape(samples, SEQ, KQ),
        precision=lax.Precision.HIGHEST,
    )
    partial_value = jnp.concatenate(
        [first_matrix.reshape(samples, KP * KQ), second_matrix.reshape(samples, KP * KQ)], axis=1
    )
    features = lax.psum(partial_value, "mp")
    every_target = lax.all_gather(targets, ("dp", "mp"), axis=1, tiled=True)
    inner = jnp.dot(features, every_target.T, precision=lax.Precision.HIGHEST)
    sample_squares = jnp.sum(features * features, axis=1)
    target_squares = jnp.sum(every_target * every_target, axis=1)
    sample_rms = jnp.sqrt(sample_squares / FEAT + epsilon)
    target_rms = jnp.sqrt(target_squares / FEAT + epsilon)
    return inner / (math.sqrt(FEAT) * sample_rms[:, None] * target_rms[None, :])


def solution(mesh):
    in_specs = (
        P("dp", "mp"),
        P("dp", "mp"),
        P("dp"),
        P(None, "mp"),
        P("mp", None),
        P(None, "mp", None),
        P(),
        P(None, ("dp", "mp")),
    )
    out_specs = P("dp", None)
    return jax.shard_map(
        on_device, mesh=mesh, in_specs=in_specs, out_specs=out_specs, check_vma=False
    )
```

profile of v0, /device:TPU:0, one launch (start us, length us, event | category | flops | bytes accessed | tf_op | source)
XLA Modules:
  0.0 130.8 jit_solution(16499203396642434931)
XLA Ops:
  7.4 0.8 convert_element_type.2
  8.1 7.2 %broadcast_multiply_fusion = bf16[2048,2048]{1,0:T(8,128)(2,1)} fusion(bf16[2048,2048]{1,0:T(8,128)(2,1)} %param.9, bf16[2048]{0:T(1024)(128)(2,1)S(1)} %convert_element_type.2), kind=kLoop, calls=%fused_computation | loop fusion | flops 4194304 | bytes 16781312 | tf_op jit(solution)/shard_map/mul | solution.py:29
  15.4 6.9 %fusion.13 = f32[2048,128]{1,0:T(8,128)} fusion(bf16[2048,2048]{1,0:T(8,128)(2,1)} %param.8, bf16[128,2048]{1,0:T(8,128)(2,1)S(1)} %copy-done), kind=kOutput, calls=%fused_computation.22 | convolution fusion | flops 1073741824 | bytes 9961472 | tf_op jit(solution)/shard_map/dot_general | solution.py:32
  22.3 3.4 %fusion.12 = f32[2048,128]{1,0:T(8,128)} fusion(bf16[2048,2048]{1,0:T(8,128)(2,1)S(1)} %copy-done.1, bf16[2048,128]{1,0:T(8,128)(2,1)S(1)} %copy-done.7), kind=kOutput, calls=%fused_computation.21 | convolution fusion | flops 1073741824 | bytes 9961472 | tf_op jit(solution)/shard_map/dot_general | solution.py:35
  25.7 0.2 all-reduce.4.cloned.1.call-start
  25.9 6.1 %fusion = f32[8,256,256]{2,1,0:T(8,128)S(1)} fusion(bf16[8,256,2048]{2,1,0:T(8,128)(2,1)} %bitcast.34, bf16[2,2048,256]{2,1,0:T(8,128)(2,1)} %param.13), kind=kOutput, calls=%fused_computation.5 | convolution fusion | flops 2147483648 | bytes 11534336 | tf_op jit(solution)/shard_map/dot_general | solution.py:46
  32.1 7.8 %fusion.2 = f32[8,256,256]{2,1,0:T(8,128)} fusion(bf16[8,256,2048]{2,1,0:T(8,128)(2,1)} %bitcast.37, bf16[2,2048,256]{2,1,0:T(8,128)(2,1)S(1)} %copy-done.6), kind=kOutput, calls=%fused_computation.7 | convolution fusion | flops 2147483648 | bytes 11534336 | tf_op jit(solution)/shard_map/dot_general | solution.py:43
  39.9 10.0 %all-reduce.6.cloned.1.call-done = (f32[8,256,128]{2,1,0:T(8,128)}, f32[8,256,128]{2,1,0:T(8,128)}) async-done(((f32[8,256,128]{2,1,0:T(8,128)}, f32[8,256,128]{2,1,0:T(8,128)}), (f32[8,256,128]{2,1,0:T(8,128)}, f32[8,256,128]{2,1,0:T(8,128)})) %all-reduce.6.cloned.1.call-update) | async-done | bytes 2097168 | tf_op jit(solution)/shard_map/psum | solution.py:38
  49.8 1.8 %fusion.6 = f32[8,256,16]{1,2,0:T(8,128)S(1)} fusion(f32[8,256,128]{2,1,0:T(8,128)} %get-tuple-element.5, bf16[2,128,16]{1,2,0:T(8,128)(2,1)S(1)} %copy-done.5), kind=kOutput, calls=%fused_computation.13 | convolution fusion | flops 50331648 | bytes 1183744 | tf_op jit(solution)/shard_map/dot_general | solution.py:42
  51.6 1.2 convolution_multiply_fusion
  52.9 0.3 copy.10
  53.2 0.6 reshape.28
  53.8 0.3 copy-done.4
  54.1 0.6 fusion.8
  54.7 2.8 %convolution_multiply_fusion.1 = f32[8,256,16]{1,2,0:T(8,128)S(1)} fusion(f32[8,256,256]{2,1,0:T(8,128)} %fusion.2, f32[8,256,16]{1,2,0:T(8,128)S(1)} %fusion.8), kind=kOutput, calls=%fused_computation.3 | convolution fusion | flops 100696064 | bytes 2359296 | tf_op jit(solution)/shard_map/stk,stq->skq/dot_general | solution.py:49
  57.5 0.3 copy.9
  57.8 0.6 reshape.27
  58.4 0.7 pad_maximum_fusion
  59.2 0.5 all-gather.2.cloned.1.call-update
  59.8 19.0 %all-reduce.4.cloned.1.call-done = f32[8,8192]{1,0:T(8,128)} async-done(((f32[8,8192]{1,0:T(8,128)}), f32[8,8192]{1,0:T(8,128)}) %all-reduce.4.cloned.1.call-update) | async-done | bytes 262160 | tf_op jit(solution)/shard_map/psum | solution.py:64
  78.8 1.2 multiply_reduce_fusion.1
  80.0 38.8 %all-gather.2.cloned.1.call-done = f32[64,8192]{1,0:T(8,128)} async-done(((f32[64,256]{1,0:T(8,128)}), f32[64,8192]{1,0:T(8,128)}) %all-gather.2.cloned.1.call-update) | async-done | bytes 2097168 | tf_op jit(solution)/shard_map/all_gather | solution.py:65
  118.8 2.0 %multiply_reduce_fusion = f32[64]{0:T(128)S(1)} fusion(f32[64,8192]{1,0:T(8,128)} %all-gather.2.cloned.1.call-done), kind=kLoop, calls=%fused_computation.1 | loop fusion | flops 1048512 | bytes 2097408 | tf_op jit(solution)/shard_map/reduce_sum | solution.py:68
  121.0 2.3 %convolution_divide_fusion = f32[8,64]{1,0:T(8,128)} fusion(f32[8,8192]{1,0:T(8,128)S(1)} %copy-done.3, f32[64,8192]{1,0:T(8,128)S(1)} %copy-done.2, f32[64]{0:T(128)S(1)} %add_sqrt_fusion, f32[8]{0:T(128)S(1)} %sqrt_multiply_fusion), kind=kOutput, calls=%fused_computation.4 | convolution fusion | flops 50332672 | bytes 2361632 | tf_op jit(solution)/shard_map/dot_general | solution.py:66
  (21 shorter events, 0.3 us)
Async XLA Ops:
  7.4 8.0 %copy-start = (bf16[128,2048]{1,0:T(8,128)(2,1)S(1)}, bf16[128,2048]{1,0:T(8,128)(2,1)}, u32[]{:S(2)}) copy-start(bf16[128,2048]{1,0:T(8,128)(2,1)} %param.11) | copy-start | bytes 1572868
  7.4 42.5 %all-reduce.6.cloned.1.call-start = ((), (), s32[]{:S(2)}) async-start(), calls=%async_computation.2 | async-start | bytes 4194304 | tf_op jit(solution)/shard_map/psum | solution.py:38
  15.4 6.9 %copy-start.1 = (bf16[2048,2048]{1,0:T(8,128)(2,1)S(1)}, bf16[2048,2048]{1,0:T(8,128)(2,1)}, u32[]{:S(2)}) copy-start(bf16[2048,2048]{1,0:T(8,128)(2,1)} %broadcast_multiply_fusion) | copy-start | bytes 25165828
  15.4 6.9 %copy-start.7 = (bf16[2048,128]{1,0:T(8,128)(2,1)S(1)}, bf16[2048,128]{1,0:T(8,128)(2,1)}, u32[]{:S(2)}) copy-start(bf16[2048,128]{1,0:T(8,128)(2,1)} %param.12) | copy-start | bytes 1572868
  25.7 53.1 %all-reduce.4.cloned.1.call-start = ((), (), s32[]{:S(2)}) async-start(), calls=%async_computation | async-start | bytes 524288 | tf_op jit(solution)/shard_map/psum | solution.py:64
  25.9 6.1 %copy-start.6 = (bf16[2,2048,256]{2,1,0:T(8,128)(2,1)S(1)}, bf16[2,2048,256]{2,1,0:T(8,128)(2,1)}, u32[]{:S(2)}) copy-start(bf16[2,2048,256]{2,1,0:T(8,128)(2,1)} %param.13) | copy-start | bytes 6291460
  32.1 17.8 %copy-start.5 = (bf16[2,128,16]{1,2,0:T(8,128)(2,1)S(1)}, bf16[2,128,16]{1,2,0:T(8,128)(2,1)}, u32[]{:S(2)}) copy-start(bf16[2,128,16]{1,2,0:T(8,128)(2,1)} %param.14) | copy-start | bytes 24580
  52.8 1.2 copy-start.4
  59.2 59.6 %all-gather.2.cloned.1.call-start = ((), (), s32[]{:S(2)}) async-start(), calls=%async_computation.1 | async-start | bytes 2162688 | tf_op jit(solution)/shard_map/all_gather | solution.py:65
  78.8 42.0 %copy-start.3 = (f32[8,8192]{1,0:T(8,128)S(1)}, f32[8,8192]{1,0:T(8,128)}, u32[]{:S(2)}) copy-start(f32[8,8192]{1,0:T(8,128)} %all-reduce.4.cloned.1.call-done) | copy-start | bytes 786436
  118.8 2.2 %copy-start.2 = (f32[64,8192]{1,0:T(8,128)S(1)}, f32[64,8192]{1,0:T(8,128)}, u32[]{:S(2)}) copy-start(f32[64,8192]{1,0:T(8,128)} %all-gather.2.cloned.1.call-done) | copy-start | bytes 6291460
Sparse Core Ops, SparseCore 0:
  25.8 23.9 all-reduce.5
  59.3 19.4 all-reduce.3
Sparse Core Ops, SparseCore 1:
  62.6 56.1 all-gather.1
where the time goes:
time: 131 us
  waiting for transfers between devices  68.3 us (52%)
  matrix products  32.9 us (25%)
  between operations  14.9 us (11%)
  other arithmetic  11.9 us (9%)
  local copies, waits for them, and re-layouts  2.42 us (2%)
    all_gather x1, waiting for transfers between devices, on_device(): every_target = lax.all_gather(targets, ('dp', 'mp'), axis=1, tiled=True)  38.8 us
    psum x1, waiting for transfers between devices, on_device(): features = lax.psum(partial_value, 'mp')  19 us
    psum x1, waiting for transfers between devices, on_device(): lax.psum((down_partial_gradient, up_partial_gradient), 'mp')  9.98 us
    dot_general x1, matrix products, on_device(): jnp.dot(inputs, width_projection[0], preferred_element_type=jnp.float32)  7.79 us
    mul x1, other arithmetic, on_device(): masked_gradient = cotangents * loss_token_mask.astype(jnp.bfloat16)[:, None]  7.23 us
    dot_general x1, matrix products, on_device(): jnp.dot(inputs, adapter_down_weight.T, preferred_element_type=jnp.float32)  6.87 us
    dot_general x1, matrix products, on_device(): jnp.dot(masked_gradient, width_projection[1], preferred_element_type=jnp....  6.11 us
    dot_general x1, matrix products, on_device(): jnp.dot(masked_gradient, adapter_up_weight, preferred_element_type=jnp.fl...  3.41 us
  transfers between devices with their start and end apart: 3, of which 3 were waited for; matrix products, arithmetic and copies ran while one was open for 12% of the time, Pallas kernels for 0%

commit v1 on v0

v1 whole, which is shorter than its diff:
```python
import functools
import math

import jax
import jax.numpy as jnp
from jax import lax
from jax.experimental import pallas as pl
from jax.experimental.pallas import tpu as pltpu
from jax.sharding import PartitionSpec as P

SEQ = 256
KP = 256
KQ = 16
FEAT = 8192
PLANE = 4
LAG = 2

adapter_scale = 4.0
epsilon = 1e-06

f32 = jnp.float32
bf16 = jnp.bfloat16


def split(value):
    high = value.astype(bf16)
    low = (value - high.astype(f32)).astype(bf16)
    return high, low


def kernel(
    n_dp, samples,
    x_hbm, g_hbm, mask_ref, down_hbm, up_hbm, wp_hbm, rp_ref, tgt_ref, out_ref,
    xv, gv, dv, uv, wv, w2, acol, cs, cr, ys, tp, tt, tth, ttl, fs, fr, es, er,
    xsem, gsem, wsem, zsend, zrecv, psend, csend, crecv, fsend, frecv, esend, erecv,
):
    me = lax.axis_index("dp")
    core = lax.axis_index("mp")
    lines = n_dp // PLANE
    mine_z = lax.div(me, PLANE)
    mine_p = lax.rem(me, PLANE)
    width = xv.shape[2]
    chunk = width // samples
    rows_of = n_dp * KQ

    down_copy = pltpu.make_async_copy(down_hbm, dv, wsem.at[0])
    up_copy = pltpu.make_async_copy(up_hbm, uv, wsem.at[1])
    wp_copy = pltpu.make_async_copy(wp_hbm, wv, wsem.at[2])

    def x_copy(n):
        rows = pl.ds(pl.multiple_of(n * SEQ, SEQ), SEQ)
        return pltpu.make_async_copy(x_hbm.at[rows], xv.at[n], xsem.at[n])

    def g_copy(n):
        rows = pl.ds(pl.multiple_of(n * SEQ, SEQ), SEQ)
        return pltpu.make_async_copy(g_hbm.at[rows], gv.at[n], gsem.at[n])

    down_copy.start()
    up_copy.start()
    for n in range(samples):
        x_copy(n).start()
        g_copy(n).start()
        if n == 0:
            wp_copy.start()

    def z_peer(r):
        return lax.rem(mine_z + r, lines) * PLANE + mine_p

    def p_peer(r):
        return mine_z * PLANE + lax.rem(mine_p + r, PLANE)

    barrier = pltpu.get_barrier_semaphore()
    for r in range(1, lines):
        pl.semaphore_signal(barrier, inc=1, device_id={"dp": z_peer(r)}, device_id_type=pl.DeviceIdType.MESH)
    for r in range(1, PLANE):
        pl.semaphore_signal(barrier, inc=1, device_id={"dp": p_peer(r)}, device_id_type=pl.DeviceIdType.MESH)
    pl.semaphore_signal(barrier, inc=1, device_id={"mp": 1 - core}, device_id_type=pl.DeviceIdType.MESH)

    turned = tgt_ref[...].T
    nt = tgt_ref.shape[0]
    tp[:, 0:nt] = turned
    tp[:, nt : 2 * nt] = turned
    lane = lax.broadcasted_iota(jnp.int32, (KQ, 2 * nt), 1)
    mine_rows = pl.ds(pl.multiple_of(me * KQ, KQ), KQ)
    for pair in range(KQ // 2):
        even = tp[pl.ds(2 * pair, KQ, stride=KQ), :]
        odd = tp[pl.ds(2 * pair + 1, KQ, stride=KQ), :]
        tt[mine_rows, pair * 2 * nt : (pair + 1) * 2 * nt] = jnp.where(lane < nt, even, odd)

    pl.semaphore_wait(barrier, lines - 1 + PLANE - 1 + 1)

    def shard_copy(shard, target, send):
        rows = pl.ds(pl.multiple_of(shard * KQ, KQ), KQ)
        return pltpu.make_async_remote_copy(
            src_ref=tt.at[rows], dst_ref=tt.at[rows], send_sem=send, recv_sem=zrecv.at[shard],
            device_id={"dp": target}, device_id_type=pl.DeviceIdType.MESH,
        )

    for r in range(1, lines):
        shard_copy(me, z_peer(r), zsend.at[r]).start()

    def forward(r):
        for p in range(1, PLANE):
            shard_copy(z_peer(r), p_peer(p), psend.at[r, p]).start()

    def arrived(shard):
        shard_copy(shard, p_peer(1), zsend.at[0]).wait_recv()

    forward(0)

    down_copy.wait()
    up_copy.wait()
    first = lax.dot_general(rp_ref[1], dv[...], (((0,), (0,)), ((), ())), preferred_element_type=f32)
    high, low = split(first)
    acol[0] = jnp.concatenate([high.astype(f32), low.astype(f32)], axis=0).T.astype(bf16)
    second = jnp.dot(uv[...], rp_ref[0], preferred_element_type=f32)
    high, low = split(second)
    acol[1, :, 0:KQ] = high
    acol[1, :, KQ : 2 * KQ] = low

    def c_copy(n):
        return pltpu.make_async_remote_copy(
            src_ref=cs.at[n], dst_ref=cr.at[n], send_sem=csend.at[n], recv_sem=crecv.at[n],
            device_id={"mp": 1 - core}, device_id_type=pl.DeviceIdType.MESH,
        )

    def phase_one(n):
        x_copy(n).wait()
        down = jnp.dot(xv[n], acol[0], preferred_element_type=f32)
        g_copy(n).wait()
        up = jnp.dot(gv[n], acol[1], preferred_element_type=f32)
        down_t = down.T
        up_t = up.T
        cs[n, 0:KQ] = down_t[0:KQ] + down_t[KQ : 2 * KQ]
        cs[n, KQ : 2 * KQ] = up_t[0:KQ] + up_t[KQ : 2 * KQ]
        c_copy(n).start()

    half = samples * KQ

    def phase_two(n):
        c_copy(n).wait_recv()
        flags = mask_ref[n].astype(f32) * adapter_scale
        total = (cs[n] + cr[n]) * flags
        high, low = split(total)
        rows = pl.ds(pl.multiple_of(n * KQ, KQ), KQ)
        low_rows = pl.ds(pl.multiple_of(half + n * KQ, KQ), KQ)
        for j, (data, base) in enumerate(((xv, KQ), (gv, 0))):
            left = jnp.concatenate([high[base : base + KQ], low[base : base + KQ]], axis=0)
            out = jnp.dot(left, data[n], preferred_element_type=f32)
            y_high, y_low = split(out[0:KQ] + out[KQ : 2 * KQ])
            ys[j, rows] = y_high
            ys[j, low_rows] = y_low

    new = lax.broadcasted_iota(jnp.int32, (KP, KP), 1)
    old = lax.broadcasted_iota(jnp.int32, (KP, KP), 0)
    group = KP // 2
    wanted = lax.div(lax.rem(new, group), KQ) * (2 * KQ) + lax.div(new, group) * KQ + lax.rem(new, KQ)
    order = jnp.where(old == wanted, 1.0, 0.0).astype(bf16)

    def reorder(n):
        rows = pl.ds(pl.multiple_of(n * chunk, chunk), chunk)
        for j in range(2):
            w2[j, rows] = jnp.dot(wv[j, rows], order, preferred_element_type=f32).astype(bf16)

    def both(n, carry):
        phase_one(n)
        phase_two(n - LAG)
        return carry

    def only_one(n, carry):
        phase_one(n)
        return carry

    def only_two(n, carry):
        phase_two(n)
        return carry

    def order_step(n, carry):
        reorder(n)
        return carry

    lax.fori_loop(0, LAG, only_one, 0)
    wp_copy.wait()
    lax.fori_loop(0, samples, order_step, 0)
    near = [r for r in range(1, lines)]
    cut = LAG + (samples - LAG) // 2
    lax.fori_loop(LAG, cut, both, 0)
    for r in near:
        arrived(z_peer(r))
        forward(r)
    lax.fori_loop(cut, samples, both, 0)
    lax.fori_loop(samples - LAG, samples, only_two, 0)

    for j in range(2):
        part = jnp.dot(ys[j], w2[j], preferred_element_type=f32)
        part = part[0:half] + part[half : 2 * half]
        for p in range(2):
            fs[p, :, j * group : (j + 1) * group] = part[:, p * group : (p + 1) * group]
    f_copy = pltpu.make_async_remote_copy(
        src_ref=fs.at[1 - core], dst_ref=fr, send_sem=fsend, recv_sem=frecv,
        device_id={"mp": 1 - core}, device_id_type=pl.DeviceIdType.MESH,
    )
    f_copy.start()

    for p in range(1, PLANE):
        for z in range(lines):
            arrived(z * PLANE + lax.rem(mine_p + p, PLANE))

    cols = KQ * nt

    def split_targets(b, carry):
        rows = pl.ds(pl.multiple_of(b * KQ, KQ), KQ)
        block = tt[rows]
        high, low = split(block)
        tth[rows] = high
        ttl[rows] = low
        return carry + block[0:8] * block[0:8] + block[8:16] * block[8:16]

    squares = lax.fori_loop(0, n_dp, split_targets, jnp.zeros((8, cols), f32))
    squares = jnp.sum(squares, axis=0, keepdims=True)

    def fold(value):
        total = value[:, 0 : 2 * nt]
        for piece in range(1, KQ // 2):
            total = total + value[:, piece * 2 * nt : (piece + 1) * 2 * nt]
        return total

    squares = fold(squares)
    es[16:24] = jnp.broadcast_to(squares, (8, 2 * nt))

    f_copy.wait()
    features = fs[core] + fr[...]
    high, low = split(features)
    inner = (
        jnp.dot(high, tth[...], preferred_element_type=f32)
        + jnp.dot(low, tth[...], preferred_element_type=f32)
        + jnp.dot(high, ttl[...], preferred_element_type=f32)
    )
    row_q = lax.rem(lax.broadcasted_iota(jnp.int32, (half, cols), 0), KQ)
    col_q = lax.div(lax.broadcasted_iota(jnp.int32, (half, cols), 1), nt)
    inner = jnp.where(row_q == col_q, inner, 0.0)
    inner = jnp.sum(inner.reshape(samples, KQ, cols), axis=1)
    es[0:8] = fold(inner)
    power = jnp.sum((features * features).reshape(samples, KQ, KP), axis=1)
    es[8:16] = power[:, 0 : KP // 2] + power[:, KP // 2 :]
    e_copy = pltpu.make_async_remote_copy(
        src_ref=es, dst_ref=er, send_sem=esend, recv_sem=erecv,
        device_id={"mp": 1 - core}, device_id_type=pl.DeviceIdType.MESH,
    )
    e_copy.start()
    for r in range(1, lines):
        shard_copy(me, z_peer(r), zsend.at[r]).wait_send()
    for r in range(lines):
        for p in range(1, PLANE):
            shard_copy(z_peer(r), p_peer(p), psend.at[r, p]).wait_send()
    for n in range(samples):
        c_copy(n).wait_send()
    e_copy.wait()
    total = es[...] + er[...]
    sample_rms = jnp.sqrt(jnp.sum(total[8:16], axis=1, keepdims=True) / FEAT + epsilon)
    target_squares = total[16:24, 0:nt] + total[16:24, nt : 2 * nt]
    target_rms = jnp.sqrt(target_squares / FEAT + epsilon)
    product = total[0:8, 0:nt] + total[0:8, nt : 2 * nt]
    out_ref[...] = product / (math.sqrt(FEAT) * sample_rms * target_rms)


def fused(n_dp, inputs, cotangents, loss_token_mask, adapter_down_weight, adapter_up_weight,
          width_projection, rank_projection, targets):
    samples = inputs.shape[0] // SEQ
    width = inputs.shape[1]
    rank = adapter_down_weight.shape[0]
    nt = targets.shape[0]
    any_spec = pl.BlockSpec(memory_space=pl.ANY)
    vmem = pl.BlockSpec(memory_space=pltpu.VMEM)
    dma = pltpu.SemaphoreType.DMA
    lines = n_dp // PLANE
    return pl.pallas_call(
        functools.partial(kernel, n_dp, samples),
        out_shape=jax.ShapeDtypeStruct((samples, nt), f32),
        in_specs=[any_spec, any_spec, vmem, any_spec, any_spec, any_spec, vmem, vmem],
        out_specs=vmem,
        scratch_shapes=[
            pltpu.VMEM((samples, SEQ, width), bf16),
            pltpu.VMEM((samples, SEQ, width), bf16),
            pltpu.VMEM((rank, width), bf16),
            pltpu.VMEM((width, rank), bf16),
            pltpu.VMEM((2, width, KP), bf16),
            pltpu.VMEM((2, width, KP), bf16),
            pltpu.VMEM((2, width, 2 * KQ), bf16),
            pltpu.VMEM((samples, 2 * KQ, SEQ), f32),
            pltpu.VMEM((samples, 2 * KQ, SEQ), f32),
            pltpu.VMEM((2, 2 * samples * KQ, width), bf16),
            pltpu.VMEM((KQ * KQ, 2 * nt), f32),
            pltpu.VMEM((n_dp * KQ, KQ * nt), f32),
            pltpu.VMEM((n_dp * KQ, KQ * nt), bf16),
            pltpu.VMEM((n_dp * KQ, KQ * nt), bf16),
            pltpu.VMEM((2, samples * KQ, KP), f32),
            pltpu.VMEM((samples * KQ, KP), f32),
            pltpu.VMEM((24, 2 * nt), f32),
            pltpu.VMEM((24, 2 * nt), f32),
            dma((samples,)), dma((samples,)), dma((3,)),
            dma((lines,)), dma((n_dp,)), dma((lines, PLANE)),
            dma((samples,)), dma((samples,)), dma, dma, dma, dma,
        ],
        compiler_params=pltpu.CompilerParams(
            collective_id=0, has_side_effects=True, vmem_limit_bytes=56 << 20
        ),
        name="influence",
    )(inputs, cotangents, loss_token_mask.reshape(samples, 1, SEQ), adapter_down_weight,
      adapter_up_weight, width_projection, rank_projection, targets)


def general(inputs, cotangents, loss_token_mask, adapter_down_weight, adapter_up_weight,
            width_projection, rank_projection, targets):
    samples = inputs.shape[0] // SEQ
    masked_gradient = cotangents * loss_token_mask.astype(bf16)[:, None]
    cols_first = rank_projection[0].astype(f32)
    cols_second = rank_projection[1].astype(f32)
    down_partial = jnp.dot(inputs, adapter_down_weight.T, preferred_element_type=f32)
    up_partial = jnp.dot(masked_gradient, adapter_up_weight, preferred_element_type=f32)
    exact = lax.Precision.HIGHEST
    compact_up, compact_down = lax.psum(
        (jnp.dot(up_partial, cols_first, precision=exact), jnp.dot(down_partial, cols_second, precision=exact)), "mp"
    )
    projected_x = jnp.dot(inputs, width_projection[0], preferred_element_type=f32).reshape(samples, SEQ, KP)
    projected_g = jnp.dot(masked_gradient, width_projection[1], preferred_element_type=f32).reshape(samples, SEQ, KP)
    first = adapter_scale * jnp.einsum(
        "stk,stq->skq", projected_x, compact_up.reshape(samples, SEQ, KQ), precision=exact)
    second = adapter_scale * jnp.einsum(
        "stk,stq->skq", projected_g, compact_down.reshape(samples, SEQ, KQ), precision=exact)
    partial_value = jnp.concatenate([first.reshape(samples, -1), second.reshape(samples, -1)], axis=1)
    features = lax.psum(partial_value, "mp")
    every_target = lax.all_gather(targets, ("dp", "mp"), axis=1, tiled=True)
    inner = jnp.dot(features, every_target.T, precision=exact)
    sample_rms = jnp.sqrt(jnp.sum(features * features, axis=1) / FEAT + epsilon)
    target_rms = jnp.sqrt(jnp.sum(every_target * every_target, axis=1) / FEAT + epsilon)
    return inner / (math.sqrt(FEAT) * sample_rms[:, None] * target_rms[None, :])


def solution(mesh):
    n_dp, n_mp = mesh.shape["dp"], mesh.shape["mp"]
    fits = n_mp == 2 and n_dp * n_mp * KQ * KQ == FEAT

    def on_device(*args):
        eight = args[0].shape[0] == 8 * SEQ
        return fused(n_dp, *args) if fits and eight else general(*args)

    in_specs = (
        P("dp", "mp"), P("dp", "mp"), P("dp"), P(None, "mp"), P("mp", None), P(None, "mp", None), P(),
        P(None, ("dp", "mp")),
    )
    return jax.shard_map(on_device, mesh=mesh, in_specs=in_specs, out_specs=P("dp", None), check_vma=False)
```

time: 131 us -> 32.3 us (0.25)
  waiting for transfers between devices: 68.3 us -> 0 us
  matrix products: 32.9 us -> 0 us
  Pallas kernels: 0 us -> 29.3 us
  between operations: 14.9 us -> 0.01 us
  other arithmetic: 11.9 us -> 0 us
    all_gather x1 -> x0, waiting for transfers between devices: 38.8 us -> none  [on_device(): every_target = lax.all_gather(targets, ('dp', 'mp'), axis=1, tiled=True)]
    dot_general x9 -> x0, matrix products: 32.9 us -> none  [the longest x1 7.79 us: on_device(): jnp.dot(inputs, width_projection[0], preferred_element_type=jnp.float32)]
    pallas_call x0 -> x1, Pallas kernels: none -> 29.3 us  [fused(): pl.pallas_call(functools.partial(kernel, n_dp, samples), out_shape=jax.Sh...]
    psum x2 -> x0, waiting for transfers between devices: 29 us -> none  [the longest x1 19 us: on_device(): features = lax.psum(partial_value, 'mp')]
    mul x2 -> x0, other arithmetic: 7.24 us -> none  [the longest x1 7.23 us: on_device(): masked_gradient = cotangents * loss_token_mask.astype(jnp.bfloat16)[:, None]]
    reduce_sum x2 -> x0, other arithmetic: 3.18 us -> none  [the longest x1 1.98 us: on_device(): target_squares = jnp.sum(every_target * every_target, axis=1)]
    unnamed x16 -> x2, local copies, waits for them, and re-layouts: 0.5 us -> 2.69 us
  transfers between devices with their start and end apart: 3 -> 0, of which waited for: 3 -> 0; matrix products, arithmetic and copies ran while one was open for 12% -> 0% of each run, Pallas kernels for 0% -> 0%
where the time goes in v1:
time: 32.3 us; the launch traced here: 32 us
  Pallas kernels  29.3 us (91%)
  local copies, waits for them, and re-layouts  2.69 us (8%)
    pallas_call x1, Pallas kernels, fused(): pl.pallas_call(functools.partial(kernel, n_dp, samples), out_shape=jax.Sh...  29.3 us
    unnamed x2, local copies, waits for them, and re-layouts  2.69 us

profile of v1, /device:TPU:0, one launch (start us, length us, event | category | flops | bytes accessed | tf_op | source)
XLA Modules:
  0.0 32.0 jit_solution(10354986128002135890)
XLA Ops:
  0.0 1.4 %copy.9.rp_ref = bf16[2,128,16]{2,1,0:T(8,128)(2,1)} copy(bf16[2,128,16]{1,2,0:T(8,128)(2,1)} %param.14) | data formatting | bytes 16384 | tf_op args[6]
  1.4 29.3 %influence.1 = f32[8,64]{1,0:T(8,128)} custom-call(bf16[2048,2048]{1,0:T(8,128)(2,1)} %x_hbm.1, bf16[2048,2048]{1,0:T(8,128)(2,1)} %g_hbm.1, s32[8,1,256]{2,1,0:T(1,128)} %bitcast.1, bf16[128,2048]{1,0:T(8,128)(2,1)} %down_hbm.1, bf16[2048,128]{1,0:T(8,128)(2,1)} %up_hbm.1, bf16[2,2048,256]{2,1,0:T(8,128)(2,1)} %wp_hbm.1, bf16[2,128,16]{2,1,0:T(8,128)(2,1)} %copy.9.rp_ref, ...), custom_call_target="tpu_custom_call" | custom-call | tf_op jit(solution)/shard_map/influence/pallas_call | solution.py:277
  30.7 1.3 %copy.11 = f32[8,64]{1,0:T(8,128)} copy(f32[8,64]{1,0:T(8,128)} %influence.1) | data formatting | bytes 4096

commit v2 on v1

v2 whole, which is shorter than its diff:
```python
import functools
import math

import jax
import jax.numpy as jnp
from jax import lax
from jax.experimental import pallas as pl
from jax.experimental.pallas import tpu as pltpu
from jax.sharding import PartitionSpec as P

SEQ = 256
KP = 256
KQ = 16
FEAT = 8192
PLANE = 4
LAG = 2

adapter_scale = 4.0
epsilon = 1e-06

f32 = jnp.float32
bf16 = jnp.bfloat16


def split(value):
    high = value.astype(bf16)
    low = (value - high.astype(f32)).astype(bf16)
    return high, low


def kernel(
    n_dp, samples,
    x_hbm, g_hbm, mask_ref, down_hbm, up_hbm, wp_hbm, rp_ref, tgt_ref, out_ref,
    xv, gv, dv, uv, wv, acol, cs, cr, ys, tp, tt, fs, fr, es, er,
    xsem, gsem, wsem, zsend, zrecv, csend, crecv, fsend, frecv, esend, erecv,
):
    me = lax.axis_index("dp")
    core = lax.axis_index("mp")
    lines = n_dp // PLANE
    group = 2 * PLANE
    mine_z = lax.div(me, PLANE)
    mine_p = lax.rem(me, PLANE)
    place = mine_p * 2 + core
    nt = tgt_ref.shape[0]
    cols = KQ * nt
    half = samples * KQ // 2

    down_copy = pltpu.make_async_copy(down_hbm, dv, wsem.at[0])
    up_copy = pltpu.make_async_copy(up_hbm, uv, wsem.at[1])
    wp_copy = pltpu.make_async_copy(wp_hbm, wv, wsem.at[2])

    def x_copy(n):
        rows = pl.ds(pl.multiple_of(n * SEQ, SEQ), SEQ)
        return pltpu.make_async_copy(x_hbm.at[rows], xv.at[n], xsem.at[n])

    def g_copy(n):
        rows = pl.ds(pl.multiple_of(n * SEQ, SEQ), SEQ)
        return pltpu.make_async_copy(g_hbm.at[rows], gv.at[n], gsem.at[n])

    down_copy.start()
    up_copy.start()
    for n in range(samples):
        x_copy(n).start()
        g_copy(n).start()
    wp_copy.start()

    def z_peer(r):
        return {"dp": lax.rem(mine_z + r, lines) * PLANE + mine_p}

    def p_peer(r):
        there = lax.rem(place + r, group)
        return {"dp": mine_z * PLANE + lax.div(there, 2), "mp": lax.rem(there, 2)}

    mesh_ids = pl.DeviceIdType.MESH
    barrier = pltpu.get_barrier_semaphore()
    for r in range(1, lines):
        pl.semaphore_signal(barrier, inc=1, device_id=z_peer(r), device_id_type=mesh_ids)
    for r in range(1, group):
        pl.semaphore_signal(barrier, inc=1, device_id=p_peer(r), device_id_type=mesh_ids)

    turned = tgt_ref[...].T
    tp[:, 0:nt] = turned
    tp[:, nt : 2 * nt] = turned
    lane = lax.broadcasted_iota(jnp.int32, (KQ, 2 * nt), 1)
    for pair in range(KQ // 2):
        even = tp[pl.ds(2 * pair, KQ, stride=KQ), :]
        odd = tp[pl.ds(2 * pair + 1, KQ, stride=KQ), :]
        tt[mine_z, :, pair * 2 * nt : (pair + 1) * 2 * nt] = jnp.where(lane < nt, even, odd)

    down_copy.wait()
    first = jnp.dot(rp_ref[1], dv[...], preferred_element_type=f32)
    high, low = split(first)
    acol[0] = jnp.concatenate([high.astype(f32), low.astype(f32)], axis=0).T.astype(bf16)
    up_copy.wait()
    second = lax.dot_general(uv[...], rp_ref[0], (((1,), (1,)), ((), ())), preferred_element_type=f32)
    high, low = split(second)
    acol[1, :, 0:KQ] = high
    acol[1, :, KQ : 2 * KQ] = low

    pl.semaphore_wait(barrier, lines - 1 + group - 1)

    def shard_copy(r):
        return pltpu.make_async_remote_copy(
            src_ref=tt.at[mine_z], dst_ref=tt.at[mine_z], send_sem=zsend.at[r], recv_sem=zrecv.at[r],
            device_id=z_peer(r), device_id_type=mesh_ids,
        )

    for r in range(1, lines):
        shard_copy(r).start()

    def c_copy(n):
        return pltpu.make_async_remote_copy(
            src_ref=cs.at[n], dst_ref=cr.at[n], send_sem=csend.at[n], recv_sem=crecv.at[n],
            device_id={"mp": 1 - core}, device_id_type=mesh_ids,
        )

    def phase_one(n):
        x_copy(n).wait()
        down = jnp.dot(xv[n], acol[0], preferred_element_type=f32)
        g_copy(n).wait()
        up = jnp.dot(gv[n], acol[1], preferred_element_type=f32)
        down_t = down.T
        up_t = up.T
        cs[n, 0:KQ] = down_t[0:KQ] + down_t[KQ : 2 * KQ]
        cs[n, KQ : 2 * KQ] = up_t[0:KQ] + up_t[KQ : 2 * KQ]
        c_copy(n).start()

    def phase_two(n):
        c_copy(n).wait_recv()
        flags = mask_ref[n].astype(f32) * adapter_scale
        total = (cs[n] + cr[n]) * flags
        high, low = split(total)
        part = lax.div(n, samples // 2)
        start = lax.rem(n, samples // 2) * KQ
        rows = pl.ds(pl.multiple_of(start, KQ), KQ)
        low_rows = pl.ds(pl.multiple_of(half + start, KQ), KQ)
        for j, (data, base) in enumerate(((xv, KQ), (gv, 0))):
            left = jnp.concatenate([high[base : base + KQ], low[base : base + KQ]], axis=0)
            out = jnp.dot(left, data[n], preferred_element_type=f32)
            y_high, y_low = split(out[0:KQ] + out[KQ : 2 * KQ])
            ys[j, part, rows] = y_high
            ys[j, part, low_rows] = y_low

    def both(n, carry):
        phase_one(n)
        phase_two(n - LAG)
        return carry

    def only_one(n, carry):
        phase_one(n)
        return carry

    def only_two(n, carry):
        phase_two(n)
        return carry

    def f_copy(h, r):
        return pltpu.make_async_remote_copy(
            src_ref=fs.at[h, lax.rem(place + r, group)], dst_ref=fr.at[h, place],
            send_sem=fsend.at[h, r], recv_sem=frecv.at[h, r],
            device_id=p_peer(r), device_id_type=mesh_ids,
        )

    quarter = half // 2
    lane_block = lax.div(lax.broadcasted_iota(jnp.int32, (quarter, 8 * KQ), 1), KQ)

    def send_features(h):
        slabs = []
        for j in range(2):
            out = jnp.dot(ys[j, h], wv[j], preferred_element_type=f32)
            out = out[0:half] + out[half : 2 * half]
            for g in range(2):
                for line in range(2):
                    slab = out[g * quarter : (g + 1) * quarter, line * 8 * KQ : (line + 1) * 8 * KQ]
                    slabs.append((g * 4 + j * 2 + line, slab))
        for e in range(group):
            piece = None
            for block, slab in slabs:
                shift = (block - e) % 8 * KQ
                moved = pltpu.roll(slab, shift, 1) if shift else slab
                piece = moved if piece is None else jnp.where(lane_block == block, moved, piece)
            fs[h, e] = piece
        for r in range(1, group):
            f_copy(h, r).start()

    cut = LAG + samples // 2
    lax.fori_loop(0, LAG, only_one, 0)
    lax.fori_loop(LAG, cut, both, 0)
    wp_copy.wait()
    send_features(0)
    lax.fori_loop(cut, samples, both, 0)
    lax.fori_loop(samples - LAG, samples, only_two, 0)
    send_features(1)

    for r in range(1, lines):
        shard_copy(r).wait()

    def fold(value):
        total = value[:, 0 : 2 * nt]
        for piece in range(1, KQ // 2):
            total = total + value[:, piece * 2 * nt : (piece + 1) * 2 * nt]
        return total

    held = tt[...].reshape(lines * KQ, cols)
    squares = fold(jnp.sum(held * held, axis=0, keepdims=True))
    squares = jnp.broadcast_to(squares, (8, 2 * nt))
    tt_high, tt_low = split(held)
    twice_high = jnp.concatenate([tt_high, tt_high], axis=0)
    twice_low = jnp.concatenate([tt_low, tt_low], axis=0)

    fr[0, place] = fs[0, place]
    fr[1, place] = fs[1, place]
    for h in range(2):
        for r in range(1, group):
            f_copy(h, r).wait()
    stacked = []
    for p in range(PLANE):
        for h in range(2):
            total = fr[h, 2 * p] + fr[h, 2 * p + 1]
            for g in range(2):
                stacked.append(jnp.where(lax.div(lane_block, 4) == g, total, 0.0))
    stacked = jnp.concatenate(stacked, axis=0)
    power = jnp.sum((stacked * stacked).reshape(PLANE * samples, KQ, 8 * KQ), axis=1)
    high, low = split(stacked)
    inner = (
        jnp.dot(high, twice_high, preferred_element_type=f32)
        + jnp.dot(low, twice_high, preferred_element_type=f32)
        + jnp.dot(high, twice_low, preferred_element_type=f32)
    )
    shape = (PLANE * samples * KQ, cols)
    row_q = lax.rem(lax.broadcasted_iota(jnp.int32, shape, 0), KQ)
    col_q = lax.div(lax.broadcasted_iota(jnp.int32, shape, 1), nt)
    inner = jnp.where(row_q == col_q, inner, 0.0)
    inner = fold(jnp.sum(inner.reshape(PLANE * samples, KQ, cols), axis=1))

    for p in range(PLANE):
        es[p, 0:8] = inner[p * samples : (p + 1) * samples]
        es[p, 8:16] = power[p * samples : (p + 1) * samples]
        es[p, 16:24] = squares

    def e_copy(r):
        return pltpu.make_async_remote_copy(
            src_ref=es.at[lax.div(lax.rem(place + r, group), 2)], dst_ref=er.at[place],
            send_sem=esend.at[r], recv_sem=erecv.at[r],
            device_id=p_peer(r), device_id_type=mesh_ids,
        )

    for r in range(1, group):
        e_copy(r).start()
    er[place] = es[mine_p]
    for n in range(samples):
        c_copy(n).wait_send()
    for r in range(1, group):
        e_copy(r).wait()
    total = jnp.sum(er[...], axis=0)
    sample_rms = jnp.sqrt(jnp.sum(total[8:16], axis=1, keepdims=True) / FEAT + epsilon)
    target_squares = total[16:24, 0:nt] + total[16:24, nt : 2 * nt]
    target_rms = jnp.sqrt(target_squares / FEAT + epsilon)
    product = total[0:8, 0:nt] + total[0:8, nt : 2 * nt]
    out_ref[...] = product / (math.sqrt(FEAT) * sample_rms * target_rms)


def fused(n_dp, inputs, cotangents, loss_token_mask, adapter_down_weight, adapter_up_weight,
          width_projection, rank_projection, targets):
    samples = inputs.shape[0] // SEQ
    width = inputs.shape[1]
    rank = adapter_down_weight.shape[0]
    nt = targets.shape[0]
    any_spec = pl.BlockSpec(memory_space=pl.ANY)
    vmem = pl.BlockSpec(memory_space=pltpu.VMEM)
    dma = pltpu.SemaphoreType.DMA
    lines = n_dp // PLANE
    group = 2 * PLANE
    return pl.pallas_call(
        functools.partial(kernel, n_dp, samples),
        out_shape=jax.ShapeDtypeStruct((samples, nt), f32),
        in_specs=[any_spec, any_spec, vmem, any_spec, any_spec, any_spec, vmem, vmem],
        out_specs=vmem,
        scratch_shapes=[
            pltpu.VMEM((samples, SEQ, width), bf16),
            pltpu.VMEM((samples, SEQ, width), bf16),
            pltpu.VMEM((rank, width), bf16),
            pltpu.VMEM((width, rank), bf16),
            pltpu.VMEM((2, width, KP), bf16),
            pltpu.VMEM((2, width, 2 * KQ), bf16),
            pltpu.VMEM((samples, 2 * KQ, SEQ), f32),
            pltpu.VMEM((samples, 2 * KQ, SEQ), f32),
            pltpu.VMEM((2, 2, samples * KQ, width), bf16),
            pltpu.VMEM((KQ * KQ, 2 * nt), f32),
            pltpu.VMEM((lines, KQ, KQ * nt), f32),
            pltpu.VMEM((2, group, samples * KQ // 4, 8 * KQ), f32),
            pltpu.VMEM((2, group, samples * KQ // 4, 8 * KQ), f32),
            pltpu.VMEM((PLANE, 24, 2 * nt), f32),
            pltpu.VMEM((group, 24, 2 * nt), f32),
            dma((samples,)), dma((samples,)), dma((3,)),
            dma((lines,)), dma((lines,)),
            dma((samples,)), dma((samples,)),
            dma((2, group)), dma((2, group)), dma((group,)), dma((group,)),
        ],
        compiler_params=pltpu.CompilerParams(
            collective_id=0, has_side_effects=True, vmem_limit_bytes=56 << 20
        ),
        name="influence",
    )(inputs, cotangents, loss_token_mask.reshape(samples, 1, SEQ), adapter_down_weight,
      adapter_up_weight, width_projection, jnp.swapaxes(rank_projection, 1, 2), targets)


def general(inputs, cotangents, loss_token_mask, adapter_down_weight, adapter_up_weight,
            width_projection, rank_projection, targets):
    samples = inputs.shape[0] // SEQ
    masked_gradient = cotangents * loss_token_mask.astype(bf16)[:, None]
    cols_first = rank_projection[0].astype(f32)
    cols_second = rank_projection[1].astype(f32)
    down_partial = jnp.dot(inputs, adapter_down_weight.T, preferred_element_type=f32)
    up_partial = jnp.dot(masked_gradient, adapter_up_weight, preferred_element_type=f32)
    exact = lax.Precision.HIGHEST
    compact_up, compact_down = lax.psum(
        (jnp.dot(up_partial, cols_first, precision=exact), jnp.dot(down_partial, cols_second, precision=exact)), "mp"
    )
    projected_x = jnp.dot(inputs, width_projection[0], preferred_element_type=f32).reshape(samples, SEQ, KP)
    projected_g = jnp.dot(masked_gradient, width_projection[1], preferred_element_type=f32).reshape(samples, SEQ, KP)
    first = adapter_scale * jnp.einsum(
        "stk,stq->skq", projected_x, compact_up.reshape(samples, SEQ, KQ), precision=exact)
    second = adapter_scale * jnp.einsum(
        "stk,stq->skq", projected_g, compact_down.reshape(samples, SEQ, KQ), precision=exact)
    partial_value = jnp.concatenate([first.reshape(samples, -1), second.reshape(samples, -1)], axis=1)
    features = lax.psum(partial_value, "mp")
    every_target = lax.all_gather(targets, ("dp", "mp"), axis=1, tiled=True)
    inner = jnp.dot(features, every_target.T, precision=exact)
    sample_rms = jnp.sqrt(jnp.sum(features * features, axis=1) / FEAT + epsilon)
    target_rms = jnp.sqrt(jnp.sum(every_target * every_target, axis=1) / FEAT + epsilon)
    return inner / (math.sqrt(FEAT) * sample_rms[:, None] * target_rms[None, :])


def solution(mesh):
    n_dp, n_mp = mesh.shape["dp"], mesh.shape["mp"]
    fits = n_mp == 2 and n_dp * n_mp * KQ * KQ == FEAT

    def on_device(*args):
        eight = args[0].shape[0] == 8 * SEQ
        return fused(n_dp, *args) if fits and eight else general(*args)

    in_specs = (
        P("dp", "mp"), P("dp", "mp"), P("dp"), P(None, "mp"), P("mp", None), P(None, "mp", None), P(),
        P(None, ("dp", "mp")),
    )
    return jax.shard_map(on_device, mesh=mesh, in_specs=in_specs, out_specs=P("dp", None), check_vma=False)
```

time: 32.3 us -> 31.3 us (0.969)
  local copies, waits for them, and re-layouts: 2.69 us -> 1.28 us
  Pallas kernels: 29.3 us -> 29.8 us
    unnamed x2 -> x1, local copies, waits for them, and re-layouts: 2.69 us -> 1.28 us
    pallas_call x1, Pallas kernels: 29.3 us -> 29.8 us  [fused(): pl.pallas_call(functools.partial(kernel, n_dp, samples), out_shape=jax.Sh...]
where the time goes in v2:
time: 31.3 us; the launch traced here: 31.1 us
  Pallas kernels  29.8 us (95%)
  local copies, waits for them, and re-layouts  1.28 us (4%)
    pallas_call x1, Pallas kernels, fused(): pl.pallas_call(functools.partial(kernel, n_dp, samples), out_shape=jax.Sh...  29.8 us
    unnamed x1, local copies, waits for them, and re-layouts  1.28 us

profile of v2, /device:TPU:0, one launch (start us, length us, event | category | flops | bytes accessed | tf_op | source)
XLA Modules:
  0.0 31.1 jit_solution(10048059632803039422)
XLA Ops:
  0.0 29.8 %influence.1 = f32[8,64]{1,0:T(8,128)} custom-call(bf16[2048,2048]{1,0:T(8,128)(2,1)} %x_hbm.1, bf16[2048,2048]{1,0:T(8,128)(2,1)} %g_hbm.1, s32[8,1,256]{2,1,0:T(1,128)} %bitcast.2, bf16[128,2048]{1,0:T(8,128)(2,1)} %down_hbm.1, bf16[2048,128]{1,0:T(8,128)(2,1)} %up_hbm.1, bf16[2,2048,256]{2,1,0:T(8,128)(2,1)} %wp_hbm.1, bf16[2,16,128]{2,1,0:T(8,128)(2,1)} %bitcast.3, ...), custom_call_target="tpu_custom_call" | custom-call | tf_op jit(solution)/shard_map/influence/pallas_call | solution.py:274
  29.9 1.3 %copy.10 = f32[8,64]{1,0:T(8,128)} copy(f32[8,64]{1,0:T(8,128)} %influence.1) | data formatting | bytes 4096

commit v3 on v2

--- a/solution.py
+++ b/solution.py
@@ -31,8 +31,8 @@
 def kernel(
     n_dp, samples,
     x_hbm, g_hbm, mask_ref, down_hbm, up_hbm, wp_hbm, rp_ref, tgt_ref, out_ref,
-    xv, gv, dv, uv, wv, acol, cs, cr, ys, tp, tt, fs, fr, es, er,
-    xsem, gsem, wsem, zsend, zrecv, csend, crecv, fsend, frecv, esend, erecv,
+    xv, gv, dv, uv, wv, acol, cs, cr, ys, tp, tt, fs, fr, es, er, qs, qr,
+    xsem, gsem, wsem, zsend, zrecv, csend, crecv, fsend, frecv, esend, erecv, qsend, qrecv,
 ):
     me = lax.axis_index("dp")
     core = lax.axis_index("mp")
@@ -205,38 +205,45 @@
     squares = fold(jnp.sum(held * held, axis=0, keepdims=True))
     squares = jnp.broadcast_to(squares, (8, 2 * nt))
     tt_high, tt_low = split(held)
-    twice_high = jnp.concatenate([tt_high, tt_high], axis=0)
-    twice_low = jnp.concatenate([tt_low, tt_low], axis=0)
-
-    fr[0, place] = fs[0, place]
-    fr[1, place] = fs[1, place]
+    right_side = jnp.concatenate([tt_high, tt_high, tt_low, tt_low], axis=0)
+    qs[...] = squares
+
+    def q_copy(r):
+        return pltpu.make_async_remote_copy(
+            src_ref=qs, dst_ref=qr.at[place], send_sem=qsend.at[r], recv_sem=qrecv.at[r],
+            device_id=p_peer(r), device_id_type=mesh_ids,
+        )
+
+    for r in range(1, group):
+        q_copy(r).start()
+    qr[place] = squares
+
+    few = samples // 2
+    shape = (PLANE * half, cols)
+    row_q = lax.rem(lax.broadcasted_iota(jnp.int32, shape, 0), KQ)
+    col_q = lax.div(lax.broadcasted_iota(jnp.int32, shape, 1), nt)
+    left_lane = lax.broadcasted_iota(jnp.int32, (PLANE * few, 2 * nt), 1) < nt
     for h in range(2):
+        fr[h, place] = fs[h, place]
         for r in range(1, group):
             f_copy(h, r).wait()
-    stacked = []
-    for p in range(PLANE):
-        for h in range(2):
+        stacked = []
+        for p in range(PLANE):
             total = fr[h, 2 * p] + fr[h, 2 * p + 1]
             for g in range(2):
                 stacked.append(jnp.where(lax.div(lane_block, 4) == g, total, 0.0))
-    stacked = jnp.concatenate(stacked, axis=0)
-    power = jnp.sum((stacked * stacked).reshape(PLANE * samples, KQ, 8 * KQ), axis=1)
-    high, low = split(stacked)
-    inner = (
-        jnp.dot(high, twice_high, preferred_element_type=f32)
-        + jnp.dot(low, twice_high, preferred_element_type=f32)
-        + jnp.dot(high, twice_low, preferred_element_type=f32)
-    )
-    shape = (PLANE * samples * KQ, cols)
-    row_q = lax.rem(lax.broadcasted_iota(jnp.int32, shape, 0), KQ)
-    col_q = lax.div(lax.broadcasted_iota(jnp.int32, shape, 1), nt)
-    inner = jnp.where(row_q == col_q, inner, 0.0)
-    inner = fold(jnp.sum(inner.reshape(PLANE * samples, KQ, cols), axis=1))
-
-    for p in range(PLANE):
-        es[p, 0:8] = inner[p * samples : (p + 1) * samples]
-        es[p, 8:16] = power[p * samples : (p + 1) * samples]
-        es[p, 16:24] = squares
+        stacked = jnp.concatenate(stacked, axis=0)
+        power = jnp.sum((stacked * stacked).reshape(PLANE * few, KQ, 8 * KQ), axis=1)
+        high, low = split(stacked)
+        filled = (high.astype(f32) + pltpu.roll(low.astype(f32), 4 * KQ, 1)).astype(bf16)
+        inner = jnp.dot(jnp.concatenate([filled, high], axis=1), right_side, preferred_element_type=f32)
+        inner = jnp.where(row_q == col_q, inner, 0.0)
+        inner = fold(jnp.sum(inner.reshape(PLANE * few, KQ, cols), axis=1))
+        inner = inner + pltpu.roll(inner, nt, 1)
+        power = power + pltpu.roll(power, nt, 1)
+        message = jnp.where(left_lane, inner, power)
+        for p in range(PLANE):
+            es[p, h * few : (h + 1) * few] = message[p * few : (p + 1) * few]
 
     def e_copy(r):
         return pltpu.make_async_remote_copy(
@@ -251,13 +258,16 @@
     for n in range(samples):
         c_copy(n).wait_send()
     for r in range(1, group):
+        q_copy(r).wait()
+    target_squares = jnp.sum(qr[...], axis=0)
+    target_squares = target_squares[:, 0:nt] + target_squares[:, nt : 2 * nt]
+    target_rms = jnp.sqrt(target_squares / FEAT + epsilon)
+    for r in range(1, group):
         e_copy(r).wait()
     total = jnp.sum(er[...], axis=0)
-    sample_rms = jnp.sqrt(jnp.sum(total[8:16], axis=1, keepdims=True) / FEAT + epsilon)
-    target_squares = total[16:24, 0:nt] + total[16:24, nt : 2 * nt]
-    target_rms = jnp.sqrt(target_squares / FEAT + epsilon)
-    product = total[0:8, 0:nt] + total[0:8, nt : 2 * nt]
-    out_ref[...] = product / (math.sqrt(FEAT) * sample_rms * target_rms)
+    sample_squares = jnp.sum(total[:, nt : 2 * nt], axis=1, keepdims=True)
+    sample_rms = jnp.sqrt(sample_squares / FEAT + epsilon)
+    out_ref[...] = total[:, 0:nt] / (math.sqrt(FEAT) * sample_rms * target_rms)
 
 
 def fused(n_dp, inputs, cotangents, loss_token_mask, adapter_down_weight, adapter_up_weight,
@@ -290,12 +300,14 @@
             pltpu.VMEM((lines, KQ, KQ * nt), f32),
             pltpu.VMEM((2, group, samples * KQ // 4, 8 * KQ), f32),
             pltpu.VMEM((2, group, samples * KQ // 4, 8 * KQ), f32),
-            pltpu.VMEM((PLANE, 24, 2 * nt), f32),
-            pltpu.VMEM((group, 24, 2 * nt), f32),
+            pltpu.VMEM((PLANE, samples, 2 * nt), f32),
+            pltpu.VMEM((group, samples, 2 * nt), f32),
+            pltpu.VMEM((8, 2 * nt), f32),
+            pltpu.VMEM((group, 8, 2 * nt), f32),
             dma((samples,)), dma((samples,)), dma((3,)),
             dma((lines,)), dma((lines,)),
             dma((samples,)), dma((samples,)),
-            dma((2, group)), dma((2, group)), dma((group,)), dma((group,)),
+            dma((2, group)), dma((2, group)), dma((group,)), dma((group,)), dma((group,)), dma((group,)),
         ],
         compiler_params=pltpu.CompilerParams(
             collective_id=0, has_side_effects=True, vmem_limit_bytes=56 << 20

time: 31.3 us -> 30.9 us (0.987)
  Pallas kernels: 29.8 us -> 29.4 us
    pallas_call x1, Pallas kernels: 29.8 us -> 29.4 us  [fused(): pl.pallas_call(functools.partial(kernel, n_dp, samples), out_shape=jax.Sh...]
where the time goes in v3:
time: 30.9 us; the launch traced here: 30.7 us
  Pallas kernels  29.4 us (95%)
  local copies, waits for them, and re-layouts  1.28 us (4%)
    pallas_call x1, Pallas kernels, fused(): pl.pallas_call(functools.partial(kernel, n_dp, samples), out_shape=jax.Sh...  29.4 us
    unnamed x1, local copies, waits for them, and re-layouts  1.28 us

profile of v3, /device:TPU:0, one launch (start us, length us, event | category | flops | bytes accessed | tf_op | source)
XLA Modules:
  0.0 30.7 jit_solution(16938463129611394255)
XLA Ops:
  0.0 29.4 %influence.1 = f32[8,64]{1,0:T(8,128)} custom-call(bf16[2048,2048]{1,0:T(8,128)(2,1)} %x_hbm.1, bf16[2048,2048]{1,0:T(8,128)(2,1)} %g_hbm.1, s32[8,1,256]{2,1,0:T(1,128)} %bitcast.2, bf16[128,2048]{1,0:T(8,128)(2,1)} %down_hbm.1, bf16[2048,128]{1,0:T(8,128)(2,1)} %up_hbm.1, bf16[2,2048,256]{2,1,0:T(8,128)(2,1)} %wp_hbm.1, bf16[2,16,128]{2,1,0:T(8,128)(2,1)} %bitcast.3, ...), custom_call_target="tpu_custom_call" | custom-call | tf_op jit(solution)/shard_map/influence/pallas_call | solution.py:284
  29.4 1.3 %copy.10 = f32[8,64]{1,0:T(8,128)} copy(f32[8,64]{1,0:T(8,128)} %influence.1) | data formatting | bytes 4096

commit v4 on v3

--- a/solution.py
+++ b/solution.py
@@ -90,12 +90,11 @@
     down_copy.wait()
     first = jnp.dot(rp_ref[1], dv[...], preferred_element_type=f32)
     high, low = split(first)
-    acol[0] = jnp.concatenate([high.astype(f32), low.astype(f32)], axis=0).T.astype(bf16)
+    acol[0] = jnp.concatenate([high, low], axis=0)
     up_copy.wait()
-    second = lax.dot_general(uv[...], rp_ref[0], (((1,), (1,)), ((), ())), preferred_element_type=f32)
+    second = lax.dot_general(rp_ref[0], uv[...], (((1,), (1,)), ((), ())), preferred_element_type=f32)
     high, low = split(second)
-    acol[1, :, 0:KQ] = high
-    acol[1, :, KQ : 2 * KQ] = low
+    acol[1] = jnp.concatenate([high, low], axis=0)
 
     pl.semaphore_wait(barrier, lines - 1 + group - 1)
 
@@ -115,18 +114,12 @@
         )
 
     def phase_one(n):
-        x_copy(n).wait()
-        down = jnp.dot(xv[n], acol[0], preferred_element_type=f32)
-        g_copy(n).wait()
-        up = jnp.dot(gv[n], acol[1], preferred_element_type=f32)
-        down_t = down.T
-        up_t = up.T
+        down_t = lax.dot_general(acol[0], xv[n], (((1,), (1,)), ((), ())), preferred_element_type=f32)
+        up_t = lax.dot_general(acol[1], gv[n], (((1,), (1,)), ((), ())), preferred_element_type=f32)
         cs[n, 0:KQ] = down_t[0:KQ] + down_t[KQ : 2 * KQ]
         cs[n, KQ : 2 * KQ] = up_t[0:KQ] + up_t[KQ : 2 * KQ]
-        c_copy(n).start()
 
     def phase_two(n):
-        c_copy(n).wait_recv()
         flags = mask_ref[n].astype(f32) * adapter_scale
         total = (cs[n] + cr[n]) * flags
         high, low = split(total)
@@ -142,15 +135,23 @@
             ys[j, part, low_rows] = y_low
 
     def both(n, carry):
+        x_copy(n).wait()
+        g_copy(n).wait()
+        c_copy(n - LAG).wait_recv()
         phase_one(n)
         phase_two(n - LAG)
+        c_copy(n).start()
         return carry
 
     def only_one(n, carry):
+        x_copy(n).wait()
+        g_copy(n).wait()
         phase_one(n)
+        c_copy(n).start()
         return carry
 
     def only_two(n, carry):
+        c_copy(n).wait_recv()
         phase_two(n)
         return carry
 
@@ -292,7 +293,7 @@
             pltpu.VMEM((rank, width), bf16),
             pltpu.VMEM((width, rank), bf16),
             pltpu.VMEM((2, width, KP), bf16),
-            pltpu.VMEM((2, width, 2 * KQ), bf16),
+            pltpu.VMEM((2, 2 * KQ, width), bf16),
             pltpu.VMEM((samples, 2 * KQ, SEQ), f32),
             pltpu.VMEM((samples, 2 * KQ, SEQ), f32),
             pltpu.VMEM((2, 2, samples * KQ, width), bf16),

time: 30.9 us -> 29.5 us (0.955)
  Pallas kernels: 29.4 us -> 28 us
    pallas_call x1, Pallas kernels: 29.4 us -> 28 us  [fused(): pl.pallas_call(functools.partial(kernel, n_dp, samples), out_shape=jax.Sh...]
where the time goes in v4:
time: 29.5 us; the launch traced here: 29.3 us
  Pallas kernels  28 us (95%)
  local copies, waits for them, and re-layouts  1.28 us (4%)
    pallas_call x1, Pallas kernels, fused(): pl.pallas_call(functools.partial(kernel, n_dp, samples), out_shape=jax.Sh...  28 us
    unnamed x1, local copies, waits for them, and re-layouts  1.28 us

profile of v4, /device:TPU:0, one launch (start us, length us, event | category | flops | bytes accessed | tf_op | source)
XLA Modules:
  0.0 29.3 jit_solution(3286715960078588827)
XLA Ops:
  0.0 28.0 %influence.1 = f32[8,64]{1,0:T(8,128)} custom-call(bf16[2048,2048]{1,0:T(8,128)(2,1)} %x_hbm.1, bf16[2048,2048]{1,0:T(8,128)(2,1)} %g_hbm.1, s32[8,1,256]{2,1,0:T(1,128)} %bitcast.2, bf16[128,2048]{1,0:T(8,128)(2,1)} %down_hbm.1, bf16[2048,128]{1,0:T(8,128)(2,1)} %up_hbm.1, bf16[2,2048,256]{2,1,0:T(8,128)(2,1)} %wp_hbm.1, bf16[2,16,128]{2,1,0:T(8,128)(2,1)} %bitcast.3, ...), custom_call_target="tpu_custom_call" | custom-call | tf_op jit(solution)/shard_map/influence/pallas_call | solution.py:285
  28.0 1.3 %copy.10 = f32[8,64]{1,0:T(8,128)} copy(f32[8,64]{1,0:T(8,128)} %influence.1) | data formatting | bytes 4096
